TPU v7x, 512 devices: a whole 4x8x8 slice. The times are simulated.
512 devices in a mesh: row: 32 (over y_hi, z, core), col: 16 (over y_lo, x).
Axes of the slice: x: 4, y: 8 (y_hi: 2, y_lo: 4; y = y_hi * 4 + y_lo), z: 8, core: 2. Of those that a mesh axis runs over, the one named last changes fastest.
Arguments:
- stress: float32 [256, 16384], P('col', 'row'), may hold values from -2.5 to 2.5
- state: float32 [256, 8192], P('col', 'row'), may hold values from 0 to 1
- load_rate: int32 [256, 16384], P('col', 'row'), may hold values from 0 to 2047
- a_param: float32 [8192], P('row'), may hold values from 1 to 2
- b_param: float32 [8192], P('row'), may hold values from 0.25 to 1
- near_band: bfloat16 [16384, 768], P('row'), may hold values from -0.21875 to 0.21875
- u_far: bfloat16 [64, 64, 32, 256], P('row', 'col'), may hold values from -0.1875 to 0.1875
- v_far: bfloat16 [64, 64, 32, 256], P('row', 'col'), may hold values from -0.375 to 0.375
- ranks: int32 [64, 64], P('row', 'col'), may hold values from 1 to 32, as said below
Outputs:
- new_stress: float32 [256, 16384], P('col', 'row')
- new_state: float32 [256, 8192], P('col', 'row')
Inputs may be any that keep to these rules, and one draw needn't show every extreme that they name: ranks of blocks with |I - J| <= 1 are not used; blocks with |I - J| = 2 have rank 32.
All inputs are finite; a program needn't handle non-finite values.
Results may differ from a plain program's by a relative error of at most 0.0021.
Values may be sent and summed in bfloat16 or wider, within the bound.
No kernel may reach another device: no remote copies, remote signals or barrier semaphores. Data moves between devices by JAX's collectives and lax.ppermute only.
A program may use at most 64 MiB of HBM per device.

v0:
```python
import jax
import jax.numpy as jnp
from jax import lax
from jax.sharding import PartitionSpec as P

B = 128
HSTEP = 0.2
RATE_UNIT = 1.0 / 1024.0


def local(stress, state, load_rate, a_param, b_param, near_band, u_far, v_far, ranks):
    rows = lax.axis_size("row")
    row_index = lax.axis_index("row")
    col_index = lax.axis_index("col")
    block_rows, block_cols, slots, dofs = u_far.shape
    members = stress.shape[0]
    blocks = rows * block_rows
    global_rows = row_index * block_rows + jnp.arange(block_rows, dtype=jnp.int32)
    global_cols = col_index * block_cols + jnp.arange(block_cols, dtype=jnp.int32)
    distant = jnp.abs(global_rows[:, None] - global_cols[None, :]) >= 2
    active = (jnp.arange(slots, dtype=jnp.int32)[None, None, :] < ranks[:, :, None]) & distant[
        :, :, None
    ]
    v_own = jnp.where(active[..., None], v_far, 0).astype(v_far.dtype)
    v_all = lax.all_gather(jnp.swapaxes(v_own, 0, 1), "col", axis=0, tiled=True)
    u_all = lax.all_gather(jnp.swapaxes(u_far, 0, 1), "col", axis=0, tiled=True)

    def to_blocks(value):
        return jnp.swapaxes(value.reshape(members, block_rows, -1), 0, 1)

    def from_blocks(value):
        return jnp.swapaxes(value, 0, 1).reshape(members, -1)

    plate = to_blocks(load_rate.astype(jnp.float32) * RATE_UNIT)
    stress_start, state_start = (to_blocks(stress), to_blocks(state))
    direct = a_param.reshape(block_rows, 1, B)
    evolve = b_param.reshape(block_rows, 1, B)
    band = near_band.reshape(block_rows, dofs, 3, dofs)

    def tendency(stress_now, state_now):
        decay = jnp.exp(-state_now)
        rate_a = 2.0 * decay * jnp.sinh(stress_now[..., :B] / direct)
        rate_b = 2.0 * decay * jnp.sinh(stress_now[..., B:] / direct)
        drift = evolve * (decay - jnp.sqrt(rate_a * rate_a + rate_b * rate_b))
        excess = (jnp.concatenate([rate_a, rate_b], axis=2) - plate).astype(jnp.bfloat16)
        copies = jnp.broadcast_to(excess[None], (rows,) + excess.shape)
        grid = lax.all_to_all(copies, "row", 0, 0).reshape(blocks, members, dofs)
        weights = jnp.einsum("jmd,jird->jmir", grid, v_all, preferred_element_type=jnp.float32)
        weights = weights.astype(jnp.bfloat16)
        total = jnp.einsum("jmir,jird->imd", weights, u_all, preferred_element_type=jnp.float32)
        window = []
        for offset in range(-1, block_rows + 1):
            at = row_index * block_rows + offset
            block = lax.dynamic_index_in_dim(grid, jnp.clip(at, 0, blocks - 1), 0, keepdims=False)
            window.append(jnp.where((at >= 0) & (at < blocks), block, 0).astype(block.dtype))
        windows = jnp.stack([jnp.stack(window[i : i + 3]) for i in range(block_rows)])
        total = total + jnp.einsum(
            "ismd,iksd->imk", windows, band, preferred_element_type=jnp.float32
        )
        return (-total, drift)

    rate_one, drift_one = tendency(stress_start, state_start)
    stress_one = stress_start + HSTEP * rate_one
    state_one = state_start + HSTEP * drift_one
    rate_two, drift_two = tendency(stress_one, state_one)
    stress_two = 0.75 * stress_start + 0.25 * (stress_one + HSTEP * rate_two)
    state_two = 0.75 * state_start + 0.25 * (state_one + HSTEP * drift_two)
    rate_three, drift_three = tendency(stress_two, state_two)
    new_stress = stress_start / 3.0 + 2.0 / 3.0 * (stress_two + HSTEP * rate_three)
    new_state = state_start / 3.0 + 2.0 / 3.0 * (state_two + HSTEP * drift_three)
    return (from_blocks(new_stress), from_blocks(new_state))


def solution(mesh):
    return jax.shard_map(
        local,
        mesh=mesh,
        in_specs=(
            P("col", "row"),
            P("col", "row"),
            P("col", "row"),
            P("row"),
            P("row"),
            P("row", None),
            P("row", "col", None, None),
            P("row", "col", None, None),
            P("row", "col"),
        ),
        out_specs=(P("col", "row"), P("col", "row")),
        check_vma=False,
    )
```

profile of v0, /device:TPU:8, one launch (start us, length us, event | category | flops | bytes accessed | tf_op | source)
XLA Modules:
  0.0 266.0 jit_solution(15811500693297151694)
XLA Ops:
  7.2 0.0 copy-start
  7.2 0.0 copy-start.3
  7.2 0.0 all-gather.3.cloned.1.call-start
  7.3 0.8 copy.54
  8.1 0.1 abs_compare_fusion.6
  8.2 0.1 compare_and_fusion
  8.2 1.7 fusion.23
  9.9 0.0 all-gather.3.cloned.1.call-update
  9.9 0.0 all-gather.5.cloned.1.call-start
  10.0 1.6 copy.106
  11.6 0.0 all-gather.5.cloned.1.call-update
  11.6 0.8 copy.107
  12.3 0.8 convert_multiply_fusion
  13.1 0.0 copy-done
  13.1 0.8 fusion.62
  13.9 0.9 broadcast_in_dim.51
  14.7 0.0 copy-start.4
  14.7 15.2 %all-to-all-start = ((bf16[32,2,16,256]{3,2,1,0:T(8,128)(2,1)}), bf16[32,2,16,256]{3,2,1,0:T(8,128)(2,1)S(1)}, u32[]{:S(2)}, u32[]{:S(2)}) async-start(bf16[32,2,16,256]{3,2,1,0:T(8,128)(2,1)} %broadcast_in_dim.51), calls=%async_computation | async-start | bytes 1048576 | tf_op jit(solution)/shard_map/all_to_all | solution.py:47
  30.0 0.0 copy-done.3
  30.0 0.4 reshape.98
  30.3 0.0 copy-start.2
  30.4 25.7 %all-to-all-done = bf16[32,2,16,256]{3,2,1,0:T(8,128)(2,1)S(1)} async-done(((bf16[32,2,16,256]{3,2,1,0:T(8,128)(2,1)}), bf16[32,2,16,256]{3,2,1,0:T(8,128)(2,1)S(1)}, u32[]{:S(2)}, u32[]{:S(2)}) %all-to-all-start) | async-done | bytes 524320 | tf_op jit(solution)/shard_map/all_to_all | solution.py:47
  56.1 0.3 convolution_bitcast_fusion.2
  56.4 40.5 %all-gather.3.cloned.1.call-done = bf16[64,2,32,256]{3,2,1,0:T(8,128)(2,1)} async-done(((bf16[4,2,32,256]{3,2,1,0:T(8,128)(2,1)}), bf16[64,2,32,256]{3,2,1,0:T(8,128)(2,1)}) %all-gather.3.cloned.1.call-update) | async-done | bytes 2097168 | tf_op jit(solution)/shard_map/all_gather | solution.py:25
  97.0 85.0 %all-gather.5.cloned.1.call-done = bf16[64,2,32,256]{3,2,1,0:T(8,128)(2,1)} async-done(((bf16[4,2,32,256]{3,2,1,0:T(8,128)(2,1)}), bf16[64,2,32,256]{3,2,1,0:T(8,128)(2,1)}) %all-gather.5.cloned.1.call-update) | async-done | bytes 2097168 | tf_op jit(solution)/shard_map/all_gather | solution.py:26
  182.0 0.0 copy-done.2
  182.0 0.0 copy-done.4
  182.0 0.0 copy-start.5
  182.1 0.0 copy-start.6
  182.1 4.0 %fusion.73 = (f32[2,16,256]{2,1,0:T(8,128)S(1)}, f32[2,16,256]{2,1,0:T(8,128)S(1)}) fusion(f32[2,2,8,256]{3,2,1,0:T(8,128)S(1)} %bitcast.238, f32[2,16,256]{2,1,0:T(8,128)S(1)} %convolution_bitcast_fusion.2, bf16[64,2,32,256]{3,2,1,0:T(8,128)(2,1)} %all-gather.5.cloned.1.call-done, bf16[64,16,256,1]{2,1,3,0:T(8,128)(2,1)S(1)} %bitcast.232, ...), kind=kOutput, calls=%fused_computation.132 | convolution fusion | flops 67207168 | bytes 4849664 | tf_op jit(solution)/shard_map/jmir,jird->imd/dot_general | solution.py:50
  186.1 0.0 copy-start.1
  186.1 0.0 copy-done.5
  186.1 0.0 copy-done.6
  186.1 0.1 fusion.65
  186.2 0.1 broadcast_in_dim.55
  186.3 34.7 %all_to_all.15 = bf16[32,2,16,256]{3,2,1,0:T(8,128)(2,1)S(1)} all-to-all(bf16[32,2,16,256]{3,2,1,0:T(8,128)(2,1)S(1)} %broadcast_in_dim.55), channel_id=1, replica_groups=mesh['row'=32,'col'=16] {'row'}, dimensions={0} | all-to-all | bytes 1048576 | tf_op jit(solution)/shard_map/all_to_all | solution.py:47
  221.0 1.5 convolution_bitcast_fusion.1
  222.6 0.0 copy-done.1
  222.6 3.4 %multiply_add_fusion = (f32[2,16,256]{2,1,0:T(8,128)S(1)}, f32[2,16,256]{2,1,0:T(8,128)S(1)}) fusion(f32[2,2,8,256]{3,2,1,0:T(8,128)S(1)} %bitcast.239, f32[2,16,256]{2,1,0:T(8,128)S(1)} %get-tuple-element.30, f32[2,16,256]{2,1,0:T(8,128)S(1)} %convolution_bitcast_fusion.1, bf16[64,2,32,256]{3,2,1,0:T(8,128)(2,1)} %all-gather.5.cloned.1.call-done, ...), kind=kOutput, calls=%fused_computation.55 | convolution fusion | flops 67239936 | bytes 4882432 | tf_op jit(solution)/shard_map/jmir,jird->imd/dot_general | solution.py:50
  226.0 0.1 fusion.67
  226.1 0.9 broadcast_in_dim.56
  226.9 3.9 %all-to-all-start.2 = ((bf16[32,2,16,256]{3,2,1,0:T(8,128)(2,1)}), bf16[32,2,16,256]{3,2,1,0:T(8,128)(2,1)S(1)}, u32[]{:S(2)}, u32[]{:S(2)}) async-start(bf16[32,2,16,256]{3,2,1,0:T(8,128)(2,1)} %broadcast_in_dim.56), calls=%async_computation.2 | async-start | bytes 1048576 | tf_op jit(solution)/shard_map/all_to_all | solution.py:47
  230.8 0.6 copy.108
  231.4 22.1 %all-to-all-done.2 = bf16[32,2,16,256]{3,2,1,0:T(8,128)(2,1)S(1)} async-done(((bf16[32,2,16,256]{3,2,1,0:T(8,128)(2,1)}), bf16[32,2,16,256]{3,2,1,0:T(8,128)(2,1)S(1)}, u32[]{:S(2)}, u32[]{:S(2)}) %all-to-all-start.2) | async-done | bytes 524320 | tf_op jit(solution)/shard_map/all_to_all | solution.py:47
  253.6 1.5 convolution_bitcast_fusion
  255.1 3.4 %fusion.11 = f32[2,2,8,256]{3,2,1,0:T(8,128)S(1)} fusion(f32[2,16,256]{2,1,0:T(8,128)S(1)} %convolution_bitcast_fusion, bf16[64,2,32,256]{3,2,1,0:T(8,128)(2,1)} %all-gather.5.cloned.1.call-done, bf16[64,16,256,1]{2,1,3,0:T(8,128)(2,1)S(1)} %bitcast.234, bf16[64,2,32,256]{3,2,1,0:T(8,128)(2,1)S(1)} %copy-done.1, f32[2,16,256]{2,1,0:T(8,128)S(1)} %get-tuple-element.32, ...), kind=kOutput, calls=%fused_computation.14 | convolution fusion | flops 67272704 | bytes 4882432 | tf_op jit(solution)/shard_map/jmir,jird->imd/dot_general | solution.py:50
  258.5 0.6 copy.75
  (11 shorter events, 0.1 us)
Async XLA Ops:
  7.2 5.9 %copy-start = (f32[16,256]{1,0:T(8,128)S(1)}, f32[16,256]{1,0:T(8,128)}, u32[]{:S(2)}) copy-start(f32[16,256]{1,0:T(8,128)} %param.10) | copy-start | bytes 49156
  7.2 22.8 %copy-start.3 = (bf16[512,768]{1,0:T(8,128)(2,1)S(1)}, bf16[512,768]{1,0:T(8,128)(2,1)}, u32[]{:S(2)}) copy-start(bf16[512,768]{1,0:T(8,128)(2,1)} %param.14) | copy-start | bytes 2359300
  7.2 89.8 %all-gather.3.cloned.1.call-start = ((), (), s32[]{:S(2)}) async-start(), calls=%async_computation.3 | async-start | bytes 2228224 | tf_op jit(solution)/shard_map/all_gather | solution.py:25
  9.9 172.1 %all-gather.5.cloned.1.call-start = ((), (), s32[]{:S(2)}) async-start(), calls=%async_computation.4 | async-start | bytes 2228224 | tf_op jit(solution)/shard_map/all_gather | solution.py:26
  14.7 167.3 %copy-start.4 = (f32[16,512]{1,0:T(8,128)S(1)}, f32[16,512]{1,0:T(8,128)}, u32[]{:S(2)}) copy-start(f32[16,512]{1,0:T(8,128)} %param.9) | copy-start | bytes 98308
  14.7 41.4 %all-to-all-start = ((bf16[32,2,16,256]{3,2,1,0:T(8,128)(2,1)}), bf16[32,2,16,256]{3,2,1,0:T(8,128)(2,1)S(1)}, u32[]{:S(2)}, u32[]{:S(2)}) async-start(bf16[32,2,16,256]{3,2,1,0:T(8,128)(2,1)} %broadcast_in_dim.51), calls=%async_computation | async-start | bytes 1048576 | tf_op jit(solution)/shard_map/all_to_all | solution.py:47
  30.3 151.7 %copy-start.2 = (bf16[2,256,3,256]{3,2,1,0:T(4,128)(2,1)}, bf16[2,256,3,256]{3,2,1,0:T(4,128)(2,1)S(1)}, u32[]{:S(2)}) copy-start(bf16[2,256,3,256]{3,2,1,0:T(4,128)(2,1)S(1)} %reshape.98) | copy-start | bytes 2359300
  182.0 4.1 %copy-start.5 = (f32[256]{0:T(256)S(1)}, f32[256]{0:T(256)}, u32[]{:S(2)}) copy-start(f32[256]{0:T(256)} %param.13) | copy-start | bytes 3076
  182.1 4.1 %copy-start.6 = (f32[256]{0:T(256)S(1)}, f32[256]{0:T(256)}, u32[]{:S(2)}) copy-start(f32[256]{0:T(256)} %param.12) | copy-start | bytes 3076
  186.1 36.5 %copy-start.1 = (bf16[64,2,32,256]{3,2,1,0:T(8,128)(2,1)S(1)}, bf16[64,2,32,256]{3,2,1,0:T(8,128)(2,1)}, u32[]{:S(2)}) copy-start(bf16[64,2,32,256]{3,2,1,0:T(8,128)(2,1)} %all-gather.3.cloned.1.call-done) | copy-start | bytes 6291460
  226.9 26.6 %all-to-all-start.2 = ((bf16[32,2,16,256]{3,2,1,0:T(8,128)(2,1)}), bf16[32,2,16,256]{3,2,1,0:T(8,128)(2,1)S(1)}, u32[]{:S(2)}, u32[]{:S(2)}) async-start(bf16[32,2,16,256]{3,2,1,0:T(8,128)(2,1)} %broadcast_in_dim.56), calls=%async_computation.2 | async-start | bytes 1048576 | tf_op jit(solution)/shard_map/all_to_all | solution.py:47
Sparse Core Ops, SparseCore 0:
  10.1 86.8 all-gather.2
  99.1 82.9 all-gather.4
where the time goes:
time: 267 us; the launch traced here: 266 us
  waiting for transfers between devices  173 us (65%)
  blocking collectives  34.7 us (13%)
  starting transfers between devices  19.2 us (7%)
  matrix products  14.2 us (5%)
  between operations  14.2 us (5%)
  local copies, waits for them, and re-layouts  6.56 us (2%)
  other arithmetic  3.55 us (1%)
    all_gather x1, waiting for transfers between devices, local(): u_all = lax.all_gather(jnp.swapaxes(u_far, 0, 1), 'col', axis=0, tiled=True)  85 us
    all_to_all x2, waiting for transfers between devices, tendency(): grid = lax.all_to_all(copies, 'row', 0, 0).reshape(blocks, members, dofs)  47.9 us
    all_gather x1, waiting for transfers between devices, local(): v_all = lax.all_gather(jnp.swapaxes(v_own, 0, 1), 'col', axis=0, tiled=True)  40.5 us
    all_to_all x1, blocking collectives, tendency(): grid = lax.all_to_all(copies, 'row', 0, 0).reshape(blocks, members, dofs)  34.7 us
    all_to_all x2, starting transfers between devices, tendency(): grid = lax.all_to_all(copies, 'row', 0, 0).reshape(blocks, members, dofs)  19.1 us
    dot_general x3, matrix products, tendency(): jnp.einsum('jmir,jird->imd', weights, u_all, preferred_element_type=jnp.f...  10.8 us
  transfers between devices with their start and end apart: 4, of which 4 were waited for; matrix products, arithmetic and copies ran while one was open for 2% of the time, Pallas kernels for 0%

commit v1 on v0

--- a/solution.py
+++ b/solution.py
@@ -22,7 +22,13 @@
         :, :, None
     ]
     v_own = jnp.where(active[..., None], v_far, 0).astype(v_far.dtype)
-    v_all = lax.all_gather(jnp.swapaxes(v_own, 0, 1), "col", axis=0, tiled=True)
+    xin = jnp.swapaxes(v_own, 0, 1)
+    sides = []
+    for _ in range(lax.axis_size("col")):
+        sides.append(xin)
+    state_next = jnp.stack(sides, axis=0)
+    opened = lax.all_to_all(state_next, "col", 0, 0)
+    v_all = jnp.concatenate(opened, axis=0)
     u_all = lax.all_gather(jnp.swapaxes(u_far, 0, 1), "col", axis=0, tiled=True)
 
     def to_blocks(value):

time: 267 us -> 218 us (0.82)
  the two profiles are of different devices: /device:TPU:8 before, /device:TPU:10 now
where the time goes in v1:
time: 218 us; the launch traced here: 217 us
  waiting for transfers between devices  120 us (55%)
  blocking collectives  32.9 us (15%)
  starting transfers between devices  25 us (11%)
  matrix products  14.8 us (7%)
  between operations  14.2 us (7%)
  local copies, waits for them, and re-layouts  7.26 us (3%)
  other arithmetic  3.57 us (2%)
    all_to_all x1, waiting for transfers between devices, local(): opened = lax.all_to_all(state_next, 'col', 0, 0)  53.6 us
    all_to_all x2, waiting for transfers between devices, tendency(): grid = lax.all_to_all(copies, 'row', 0, 0).reshape(blocks, members, dofs)  42.5 us
    all_to_all x1, blocking collectives, tendency(): grid = lax.all_to_all(copies, 'row', 0, 0).reshape(blocks, members, dofs)  32.9 us
    all_gather x1, waiting for transfers between devices, local(): u_all = lax.all_gather(jnp.swapaxes(u_far, 0, 1), 'col', axis=0, tiled=True)  23 us
    all_to_all x2, starting transfers between devices, tendency(): grid = lax.all_to_all(copies, 'row', 0, 0).reshape(blocks, members, dofs)  19 us
    dot_general x3, matrix products, tendency(): jnp.einsum('jmir,jird->imd', weights, u_all, preferred_element_type=jnp.f...  10.2 us
    all_to_all x1, starting transfers between devices, local(): opened = lax.all_to_all(state_next, 'col', 0, 0)  6.04 us
    dot_general x3, matrix products, tendency(): jnp.einsum('ismd,iksd->imk', windows, band, preferred_element_type=jnp.fl...  4.6 us
  transfers between devices with their start and end apart: 4, of which 4 were waited for; matrix products, arithmetic and copies ran while one was open for 3% of the time, Pallas kernels for 0%

profile of v1, /device:TPU:10, one launch (start us, length us, event | category | flops | bytes accessed | tf_op | source)
XLA Modules:
  0.0 217.4 jit_solution(14862351182916088303)
XLA Ops:
  7.2 0.0 copy-start
  7.2 0.0 copy-start.3
  7.2 0.8 copy.96
  8.0 0.8 convert_multiply_fusion
  8.8 0.0 copy-done
  8.8 0.8 fusion.61
  9.5 0.9 broadcast_in_dim.51
  10.4 15.1 %all-to-all-start = ((bf16[32,2,16,256]{3,2,1,0:T(8,128)(2,1)}), bf16[32,2,16,256]{3,2,1,0:T(8,128)(2,1)S(1)}, u32[]{:S(2)}, u32[]{:S(2)}) async-start(bf16[32,2,16,256]{3,2,1,0:T(8,128)(2,1)} %broadcast_in_dim.51), calls=%async_computation | async-start | bytes 1048576 | tf_op jit(solution)/shard_map/all_to_all | solution.py:53
  25.5 0.1 abs_compare_fusion.6
  25.6 0.8 fusion.69
  26.3 1.0 select_bitcast_fusion
  27.4 0.0 copy-done.3
  27.4 0.7 copy.95
  28.0 20.2 %all-to-all-done = bf16[32,2,16,256]{3,2,1,0:T(8,128)(2,1)S(1)} async-done(((bf16[32,2,16,256]{3,2,1,0:T(8,128)(2,1)}), bf16[32,2,16,256]{3,2,1,0:T(8,128)(2,1)S(1)}, u32[]{:S(2)}, u32[]{:S(2)}) %all-to-all-start) | async-done | bytes 524320 | tf_op jit(solution)/shard_map/all_to_all | solution.py:53
  48.3 1.6 stack.32
  49.8 0.0 copy-start.1
  49.8 6.0 %all-to-all-start.1 = ((bf16[16,4,2,32,256]{4,3,2,1,0:T(8,128)(2,1)}), bf16[16,4,2,32,256]{4,3,2,1,0:T(8,128)(2,1)S(1)}, u32[]{:S(2)}, u32[]{:S(2)}) async-start(bf16[16,4,2,32,256]{4,3,2,1,0:T(8,128)(2,1)} %stack.32), calls=%async_computation.1 | async-start | bytes 4194304 | tf_op jit(solution)/shard_map/all_to_all | solution.py:30
  55.9 0.0 copy-start.2
  55.9 0.0 all-gather.2.cloned.1.call-start
  55.9 0.7 all-gather.2.cloned.1.call-update
  56.6 0.0 copy-done.1
  56.6 1.2 reshape.104
  57.9 1.5 convolution_bitcast_fusion.2
  59.4 53.6 %all-to-all-done.1 = bf16[16,4,2,32,256]{4,3,2,1,0:T(8,128)(2,1)S(1)} async-done(((bf16[16,4,2,32,256]{4,3,2,1,0:T(8,128)(2,1)}), bf16[16,4,2,32,256]{4,3,2,1,0:T(8,128)(2,1)S(1)}, u32[]{:S(2)}, u32[]{:S(2)}) %all-to-all-start.1) | async-done | bytes 2097184 | tf_op jit(solution)/shard_map/all_to_all | solution.py:30
  112.9 23.0 %all-gather.2.cloned.1.call-done = bf16[64,2,32,256]{3,2,1,0:T(8,128)(2,1)} async-done(((bf16[4,2,32,256]{3,2,1,0:T(8,128)(2,1)}), bf16[64,2,32,256]{3,2,1,0:T(8,128)(2,1)}) %all-gather.2.cloned.1.call-update) | async-done | bytes 2097168 | tf_op jit(solution)/shard_map/all_gather | solution.py:32
  135.9 0.0 copy-done.2
  135.9 0.0 copy-start.4
  135.9 0.0 copy-start.5
  135.9 3.4 %fusion.73 = (f32[2,16,256]{2,1,0:T(8,128)S(1)}, f32[2,16,256]{2,1,0:T(8,128)S(1)}) fusion(f32[2,2,8,256]{3,2,1,0:T(8,128)S(1)} %bitcast.242, f32[2,16,256]{2,1,0:T(8,128)S(1)} %convolution_bitcast_fusion.2, bf16[64,2,32,256]{3,2,1,0:T(8,128)(2,1)} %all-gather.2.cloned.1.call-done, bf16[64,16,256,1]{2,1,3,0:T(8,128)(2,1)S(1)} %bitcast.236, ...), kind=kOutput, calls=%fused_computation.132 | convolution fusion | flops 67207168 | bytes 4849664 | tf_op jit(solution)/shard_map/jmir,jird->imd/dot_general | solution.py:56
  139.3 0.0 copy-done.4
  139.3 0.0 copy-done.5
  139.3 0.1 fusion.64
  139.4 0.1 broadcast_in_dim.55
  139.5 32.9 %all_to_all.20 = bf16[32,2,16,256]{3,2,1,0:T(8,128)(2,1)S(1)} all-to-all(bf16[32,2,16,256]{3,2,1,0:T(8,128)(2,1)S(1)} %broadcast_in_dim.55), channel_id=1, replica_groups=mesh['row'=32,'col'=16] {'row'}, dimensions={0} | all-to-all | bytes 1048576 | tf_op jit(solution)/shard_map/all_to_all | solution.py:53
  172.4 1.5 convolution_bitcast_fusion.1
  173.9 3.4 %multiply_add_fusion = (f32[2,16,256]{2,1,0:T(8,128)S(1)}, f32[2,16,256]{2,1,0:T(8,128)S(1)}) fusion(f32[2,2,8,256]{3,2,1,0:T(8,128)S(1)} %bitcast.243, f32[2,16,256]{2,1,0:T(8,128)S(1)} %get-tuple-element.30, f32[2,16,256]{2,1,0:T(8,128)S(1)} %convolution_bitcast_fusion.1, bf16[64,2,32,256]{3,2,1,0:T(8,128)(2,1)} %all-gather.2.cloned.1.call-done, ...), kind=kOutput, calls=%fused_computation.54 | convolution fusion | flops 67239936 | bytes 4882432 | tf_op jit(solution)/shard_map/jmir,jird->imd/dot_general | solution.py:56
  177.3 0.1 fusion.66
  177.4 0.9 broadcast_in_dim.56
  178.3 3.9 %all-to-all-start.3 = ((bf16[32,2,16,256]{3,2,1,0:T(8,128)(2,1)}), bf16[32,2,16,256]{3,2,1,0:T(8,128)(2,1)S(1)}, u32[]{:S(2)}, u32[]{:S(2)}) async-start(bf16[32,2,16,256]{3,2,1,0:T(8,128)(2,1)} %broadcast_in_dim.56), calls=%async_computation.3 | async-start | bytes 1048576 | tf_op jit(solution)/shard_map/all_to_all | solution.py:53
  182.2 0.6 copy.97
  182.8 22.2 %all-to-all-done.3 = bf16[32,2,16,256]{3,2,1,0:T(8,128)(2,1)S(1)} async-done(((bf16[32,2,16,256]{3,2,1,0:T(8,128)(2,1)}), bf16[32,2,16,256]{3,2,1,0:T(8,128)(2,1)S(1)}, u32[]{:S(2)}, u32[]{:S(2)}) %all-to-all-start.3) | async-done | bytes 524320 | tf_op jit(solution)/shard_map/all_to_all | solution.py:53
  205.0 1.5 convolution_bitcast_fusion
  206.6 3.4 %fusion.11 = f32[2,2,8,256]{3,2,1,0:T(8,128)S(1)} fusion(f32[2,16,256]{2,1,0:T(8,128)S(1)} %convolution_bitcast_fusion, bf16[64,2,32,256]{3,2,1,0:T(8,128)(2,1)} %all-gather.2.cloned.1.call-done, bf16[64,16,256,1]{2,1,3,0:T(8,128)(2,1)S(1)} %bitcast.238, bf16[64,2,32,256]{3,2,1,0:T(8,128)(2,1)S(1)} %bitcast.234, f32[2,16,256]{2,1,0:T(8,128)S(1)} %get-tuple-element.32, ...), kind=kOutput, calls=%fused_computation.14 | convolution fusion | flops 67272704 | bytes 4882432 | tf_op jit(solution)/shard_map/jmir,jird->imd/dot_general | solution.py:56
  210.0 0.6 copy.67
  (12 shorter events, 0.1 us)
Async XLA Ops:
  7.2 1.6 copy-start
  7.2 20.2 %copy-start.3 = (bf16[2,4,32,256]{3,2,1,0:T(8,128)(2,1)S(1)}, bf16[2,4,32,256]{3,2,1,0:T(8,128)(2,1)}, u32[]{:S(2)}) copy-start(bf16[2,4,32,256]{3,2,1,0:T(8,128)(2,1)} %param.15) | copy-start | bytes 393220
  10.4 37.9 %all-to-all-start = ((bf16[32,2,16,256]{3,2,1,0:T(8,128)(2,1)}), bf16[32,2,16,256]{3,2,1,0:T(8,128)(2,1)S(1)}, u32[]{:S(2)}, u32[]{:S(2)}) async-start(bf16[32,2,16,256]{3,2,1,0:T(8,128)(2,1)} %broadcast_in_dim.51), calls=%async_computation | async-start | bytes 1048576 | tf_op jit(solution)/shard_map/all_to_all | solution.py:53
  49.8 6.8 %copy-start.1 = (bf16[512,768]{1,0:T(8,128)(2,1)S(1)}, bf16[512,768]{1,0:T(8,128)(2,1)}, u32[]{:S(2)}) copy-start(bf16[512,768]{1,0:T(8,128)(2,1)} %param.14) | copy-start | bytes 2359300
  49.8 63.1 %all-to-all-start.1 = ((bf16[16,4,2,32,256]{4,3,2,1,0:T(8,128)(2,1)}), bf16[16,4,2,32,256]{4,3,2,1,0:T(8,128)(2,1)S(1)}, u32[]{:S(2)}, u32[]{:S(2)}) async-start(bf16[16,4,2,32,256]{4,3,2,1,0:T(8,128)(2,1)} %stack.32), calls=%async_computation.1 | async-start | bytes 4194304 | tf_op jit(solution)/shard_map/all_to_all | solution.py:30
  55.9 80.0 %copy-start.2 = (f32[16,512]{1,0:T(8,128)S(1)}, f32[16,512]{1,0:T(8,128)}, u32[]{:S(2)}) copy-start(f32[16,512]{1,0:T(8,128)} %param.9) | copy-start | bytes 98308
  55.9 80.0 %all-gather.2.cloned.1.call-start = ((), (), s32[]{:S(2)}) async-start(), calls=%async_computation.4 | async-start | bytes 2228224 | tf_op jit(solution)/shard_map/all_gather | solution.py:32
  135.9 3.4 %copy-start.4 = (f32[256]{0:T(256)S(1)}, f32[256]{0:T(256)}, u32[]{:S(2)}) copy-start(f32[256]{0:T(256)} %param.13) | copy-start | bytes 3076
  135.9 3.4 %copy-start.5 = (f32[256]{0:T(256)S(1)}, f32[256]{0:T(256)}, u32[]{:S(2)}) copy-start(f32[256]{0:T(256)} %param.12) | copy-start | bytes 3076
  178.3 26.7 %all-to-all-start.3 = ((bf16[32,2,16,256]{3,2,1,0:T(8,128)(2,1)}), bf16[32,2,16,256]{3,2,1,0:T(8,128)(2,1)S(1)}, u32[]{:S(2)}, u32[]{:S(2)}) async-start(bf16[32,2,16,256]{3,2,1,0:T(8,128)(2,1)} %broadcast_in_dim.56), calls=%async_computation.3 | async-start | bytes 1048576 | tf_op jit(solution)/shard_map/all_to_all | solution.py:53
Sparse Core Ops, SparseCore 0:
  58.8 77.0 all-gather.1
